TPU v7x, 32 devices: a whole 2x2x4 slice. The times are simulated.
32 devices in a mesh: gx: 4 (over y, core), gy: 8 (over z, x).
Axes of the slice: x: 2, y: 2, z: 4, core: 2. Of those that a mesh axis runs over, the one named last changes fastest.
Arguments:
- a_tiles: bfloat16 [4, 8, 16, 27, 128, 128], P('gx', 'gy'), may hold values from -0.5 to 0.5
- p_tiles: bfloat16 [4, 8, 16, 128, 128], P('gx', 'gy'), may hold values from -1.5 to 1.5
- neighbours: int32 [4, 8, 16, 27], P('gx', 'gy'), may hold values from 0 to 143, as said below
- groups: int32 [4, 8, 16, 27], P('gx', 'gy'), may hold values from 0 to 7
- slots: int32 [4, 8, 16, 8], P('gx', 'gy'), may hold values from 0 to 26
- aggregates: int32 [4, 8, 16], P('gx', 'gy'), may hold values from 0 to 31, as said below
Outputs:
- coarse_tiles: float32 [4, 8, 4, 27, 128, 128], P('gx', 'gy')
Inputs may be any that keep to these rules, and one draw needn't show every extreme that they name: `neighbours`: tile k of a fine row on device (x, y) names row q % 16 of device (x + q // 48 - 1, y + (q // 16) % 3 - 1), which is always on the mesh; tile 0 names the row itself. The owner of aggregate g is gy index g // 4, as its coarse row g % 4. At most 4 fine rows of one device have aggregates with one owner; in every slab one owner gets exactly 4 from every device of the slab.
All inputs are finite; a program needn't handle non-finite values.
Results may differ from a plain program's by a relative error of at most 0.005.
Values may be sent and summed in bfloat16 or wider, within the bound.
A program may use at most 128 MiB of HBM per device.

v0:
```python
import jax
import jax.numpy as jnp
from jax import lax
from jax.sharding import PartitionSpec as P

KC = 27
AGG = 4


def extended(block, sides, width):
    for axis, dim in sides:
        count = lax.axis_size(axis)
        forward = [(i, i + 1) for i in range(count - 1)]
        backward = [(target, source) for source, target in forward]
        low = lax.ppermute(
            lax.slice_in_dim(block, block.shape[dim] - width, None, axis=dim), axis, forward
        )
        high = lax.ppermute(lax.slice_in_dim(block, 0, width, axis=dim), axis, backward)
        block = jnp.concatenate([low, block, high], axis=dim)
    return block


def shards(a_tiles, p_tiles, neighbours, groups, slots, aggregates):
    row_count = a_tiles.shape[2]
    tile_size = a_tiles.shape[-1]
    touched = slots.shape[-1]
    owner_count = lax.axis_size("gy")
    row_cap = (2 * row_count + owner_count - 1) // owner_count
    slot_total = owner_count * row_cap
    coarse_rows = row_count // AGG
    a_local = a_tiles[0, 0]
    p_local = p_tiles[0, 0]
    column_local = neighbours[0, 0]
    group_local = groups[0, 0]
    slot_local = slots[0, 0]
    aggregate_local = aggregates[0, 0]
    padded = extended(p_tiles, (("gx", 0), ("gy", 1)), 1)
    p_table = padded.reshape(9 * row_count, tile_size, tile_size)

    def one_row(inputs):
        a_row, column_row, group_row, p_row = inputs
        far_tiles = jnp.take(p_table, column_row, axis=0)
        products = jnp.einsum("kab,kbc->kac", a_row, far_tiles, preferred_element_type=jnp.float32)
        picker = (group_row[:, None] == jnp.arange(touched, dtype=jnp.int32)[None, :]).astype(
            jnp.float32
        )
        summed = jnp.einsum(
            "kf,kac->fac", picker, products, precision=lax.Precision.HIGHEST
        ).astype(jnp.bfloat16)
        return jnp.einsum("ba,fbc->fac", p_row, summed, preferred_element_type=jnp.float32).astype(
            jnp.bfloat16
        )

    partials = lax.map(one_row, (a_local, column_local, group_local, p_local))
    owners = aggregate_local // coarse_rows
    local_row = aggregate_local % coarse_rows
    indices = jnp.arange(row_count, dtype=jnp.int32)
    same_owner = owners[:, None] == owners[None, :]
    earlier = indices[:, None] > indices[None, :]
    ranking = jnp.sum((same_owner & earlier).astype(jnp.int32), axis=1)
    position = owners * row_cap + ranking
    selector = jnp.arange(slot_total, dtype=jnp.int32)[:, None] == position[None, :]
    meta_ints = jnp.concatenate([(local_row + 1)[:, None], slot_local], axis=1)
    meta_sent = jnp.dot(selector.astype(jnp.int32), meta_ints)
    send_tiles = jnp.einsum(
        "sr,rfab->sfab", selector.astype(jnp.bfloat16), partials, preferred_element_type=jnp.float32
    ).astype(jnp.bfloat16)
    recv_contrib, recv_meta = (
        lax.all_to_all(send_tiles, "gy", split_axis=0, concat_axis=0, tiled=True),
        lax.all_to_all(meta_sent, "gy", split_axis=0, concat_axis=0, tiled=True),
    )
    recv_row = recv_meta[:, 0] - 1
    segment_ids = jnp.where(
        recv_row[:, None] >= 0, recv_row[:, None] * KC + recv_meta[:, 1:], coarse_rows * KC
    )
    flat_contrib = recv_contrib.reshape(slot_total * touched, tile_size, tile_size).astype(
        jnp.float32
    )
    coarse = jax.ops.segment_sum(
        flat_contrib, segment_ids.reshape(-1), num_segments=coarse_rows * KC + 1
    )
    coarse = coarse[: coarse_rows * KC]
    return coarse.reshape(1, 1, coarse_rows, KC, tile_size, tile_size)


def solution(mesh):
    return jax.shard_map(
        shards,
        mesh=mesh,
        in_specs=(
            P("gx", "gy", None, None, None, None),
            P("gx", "gy", None, None, None),
            P("gx", "gy", None, None),
            P("gx", "gy", None, None),
            P("gx", "gy", None, None),
            P("gx", "gy", None),
        ),
        out_specs=P("gx", "gy", None, None, None, None),
        check_vma=False,
    )
```

profile of v0, /device:TPU:0, one launch (start us, length us, event | category | flops | bytes accessed | tf_op | source)
XLA Modules:
  0.0 539.2 jit_solution(3211491766969522119)
XLA Ops:
  0.0 2.4 collective-permute-start
  5.3 3.2 collective-permute-done.1
  8.6 3.5 collective-permute-start.2
  17.2 8.0 %all-to-all-start = ((s32[8,4,9]{2,1,0:T(4,128)}), s32[8,4,9]{2,1,0:T(4,128)S(1)}, u32[]{:S(2)}, u32[]{:S(2)}) async-start(s32[8,4,9]{2,1,0:T(4,128)} %bitcast.13), calls=%async_computation | async-start | bytes 32768 | tf_op jit(solution)/shard_map/all_to_all | solution.py:70
  25.2 51.0 %collective-permute-done.2 = bf16[3,1,16,128,128]{4,3,2,1,0:T(8,128)(2,1)S(1)} collective-permute-done((bf16[3,1,16,128,128]{4,3,2,1,0:T(8,128)(2,1)S(1)}, bf16[3,1,16,128,128]{4,3,2,1,0:T(8,128)(2,1)S(1)}, u32[]{:S(2)}, u32[]{:S(2)}) %collective-permute-start.2) | collective-permute-done | bytes 1572896 | tf_op jit(solution)/shard_map/ppermute | solution.py:15
  76.2 3.6 pad_maximum_fusion
  79.7 164.5 %while.10 = (s32[]{:T(128)}, bf16[16,8,128,128]{2,3,1,0:T(8,128)(2,1)}, s32[16,27]{1,0:T(8,128)}, bf16[16,27,128,128]{3,2,1,0:T(8,128)(2,1)}, s32[16,27]{1,0:T(8...) while((s32[]{:T(128)}, bf16[16,8,128,128]{2,3,1,0:T(8,128)(2,1)}, ...), condition=%wide.region_2.3_spmd, body=%wide.region_1.2_spmd.sunk | while | flops 189973952 | bytes 7903735 | solution.py:54
  80.4 3.1 gather_fusion
  86.5 1.7 fusion.58
  88.3 1.7 fusion.59
  90.7 3.1 gather_fusion
  96.8 1.7 fusion.58
  98.5 1.7 fusion.59
  101.0 3.1 gather_fusion
  107.1 1.7 fusion.58
  108.8 1.7 fusion.59
  111.2 3.1 gather_fusion
  117.3 1.7 fusion.58
  119.1 1.7 fusion.59
  121.5 3.1 gather_fusion
  127.6 1.7 fusion.58
  129.4 1.7 fusion.59
  131.8 3.1 gather_fusion
  137.9 1.7 fusion.58
  139.7 1.7 fusion.59
  142.1 3.1 gather_fusion
  148.2 1.7 fusion.58
  150.0 1.7 fusion.59
  152.4 3.1 gather_fusion
  158.5 1.7 fusion.58
  160.2 1.7 fusion.59
  162.7 3.1 gather_fusion
  168.8 1.7 fusion.58
  170.5 1.8 fusion.59
  173.0 3.1 gather_fusion
  179.1 1.7 fusion.58
  180.8 1.7 fusion.59
  183.3 3.1 gather_fusion
  189.4 1.7 fusion.58
  191.1 1.7 fusion.59
  193.5 3.1 gather_fusion
  199.6 1.7 fusion.58
  201.4 1.7 fusion.59
  203.8 3.1 gather_fusion
  209.9 1.7 fusion.58
  211.7 1.7 fusion.59
  214.1 3.1 gather_fusion
  220.2 1.7 fusion.58
  222.0 1.7 fusion.59
  224.4 3.1 gather_fusion
  230.5 1.7 fusion.58
  232.2 1.7 fusion.59
  234.7 3.1 gather_fusion
  240.8 1.7 fusion.58
  242.5 1.7 fusion.59
  244.3 6.7 %copy.24 = bf16[16,8,128,128]{3,0,2,1:T(8,128)(2,1)} copy(bf16[16,8,128,128]{2,3,1,0:T(8,128)(2,1)} %get-tuple-element.42) | data formatting | bytes 8388608 | tf_op jit(solution)/shard_map/while | solution.py:54
  251.0 7.8 %convolution_convert_fusion.1 = bf16[32,8,128,128]{3,0,2,1:T(8,128)(2,1)} fusion(bf16[16,8,128,128]{3,0,2,1:T(8,128)(2,1)} %copy.24, s32[16]{0:T(128)S(1)} %multiply_add_fusion), kind=kOutput, calls=%fused_computation.32 | convolution fusion | flops 138412544 | bytes 12582976 | tf_op jit(solution)/shard_map/sr,rfab->sfab/dot_general | solution.py:65
  258.8 9.8 %copy.25 = bf16[32,8,128,128]{3,2,1,0:T(8,128)(2,1)} copy(bf16[32,8,128,128]{3,0,2,1:T(8,128)(2,1)} %convolution_convert_fusion.1) | data formatting | bytes 16777216 | tf_op jit(solution)/shard_map/convert_element_type | solution.py:67
  268.6 11.2 %all-to-all-start.1 = ((bf16[32,8,128,128]{3,2,1,0:T(8,128)(2,1)}), bf16[32,8,128,128]{3,2,1,0:T(8,128)(2,1)}, u32[]{:S(2)}, u32[]{:S(2)}) async-start(bf16[32,8,128,128]{3,2,1,0:T(8,128)(2,1)} %copy.25), calls=%async_computation.1 | async-start | bytes 16777216 | tf_op jit(solution)/shard_map/all_to_all | solution.py:69
  280.3 183.7 %all-to-all-done.1 = bf16[32,8,128,128]{3,2,1,0:T(8,128)(2,1)} async-done(((bf16[32,8,128,128]{3,2,1,0:T(8,128)(2,1)}), bf16[32,8,128,128]{3,2,1,0:T(8,128)(2,1)}, u32[]{:S(2)}, u32[]{:S(2)}) %all-to-all-start.1) | async-done | bytes 8388640 | tf_op jit(solution)/shard_map/all_to_all | solution.py:69
  464.0 11.2 %bitcast_convert_fusion = f32[256,128,128]{2,1,0:T(8,128)} fusion(bf16[32,8,128,128]{3,2,1,0:T(8,128)(2,1)} %all-to-all-done.1), kind=kLoop, calls=%fused_computation.31 | loop fusion | flops 4194304 | bytes 25165824 | tf_op jit(solution)/shard_map/convert_element_type | solution.py:76
  475.2 3.8 broadcast_in_dim.45
  479.0 53.3 %scatter_fusion = f32[109,128,128]{2,1,0:T(8,128)} fusion(f32[109,128,128]{2,1,0:T(8,128)} %broadcast_in_dim.45, s32[256]{0:T(256)S(1)} %reshape.186, f32[256,128,128]{2,1,0:T(8,128)} %bitcast_convert_fusion), kind=kCustom, calls=%fused_computation.1 | custom fusion | flops 4194304 | bytes 50332672 | tf_op jit(solution)/shard_map/scatter-add | solution.py:79
  532.3 6.9 %slice.16 = f32[108,128,128]{2,1,0:T(8,128)} slice(f32[109,128,128]{2,1,0:T(8,128)} %scatter_fusion), slice={[0:108], [0:128], [0:128]} | slice | bytes 14155776 | tf_op jit(solution)/shard_map/slice | solution.py:82
  (98 shorter events, 68.0 us)
Async XLA Ops:
  0.0 4.1 collective-permute-start
  2.4 6.1 %collective-permute-start.1 = (bf16[1,1,16,128,128]{4,3,2,1,0:T(8,128)(2,1)}, bf16[1,1,16,128,128]{4,3,2,1,0:T(8,128)(2,1)S(1)}, u32[]{:S(2)}, u32[]{:S(2)}) collective-permute-start(bf16[1,1,16,128,128]{4,3,2,1,0:T(8,128)(2,1)} %param.9), channel_id=1, source_target_pairs={{8,0},{16,8},{24,16},{9,1},{17,9},{25,17},{10,2},{18,10},{26,18},{... | collective-permute-start | bytes 1572872 | tf_op jit(solution)/shard_map/ppermute | solution.py:18
  8.6 67.5 %collective-permute-start.2 = (bf16[3,1,16,128,128]{4,3,2,1,0:T(8,128)(2,1)S(1)}, bf16[3,1,16,128,128]{4,3,2,1,0:T(8,128)(2,1)S(1)}, u32[]{:S(2)}, u32[]{:S(2)}) collective-permute-start(bf16[3,1,16,128,128]{4,3,2,1,0:T(8,128)(2,1)S(1)} %constant_dynamic-update-slice_fusion), channel_id=1, source_target_pairs={{0,1},{1,2},{2,3},{3,4},{4,5},{5,6},{6,7},{8,9},{9,10},{10,11},{11... | collective-permute-start | bytes 4718600 | tf_op jit(solution)/shard_map/ppermute | solution.py:15
  12.1 64.0 %collective-permute-start.3 = (bf16[3,1,16,128,128]{4,3,2,1,0:T(8,128)(2,1)S(1)}, bf16[3,1,16,128,128]{4,3,2,1,0:T(8,128)(2,1)}, u32[]{:S(2)}, u32[]{:S(2)}) collective-permute-start(bf16[3,1,16,128,128]{4,3,2,1,0:T(8,128)(2,1)S(1)} %constant_dynamic-update-slice_fusion), channel_id=1, source_target_pairs={{1,0},{2,1},{3,2},{4,3},{5,4},{6,5},{7,6},{9,8},{10,9},{11,10},{12... | collective-permute-start | bytes 4718600 | tf_op jit(solution)/shard_map/ppermute | solution.py:18
  17.2 251.5 %all-to-all-start = ((s32[8,4,9]{2,1,0:T(4,128)}), s32[8,4,9]{2,1,0:T(4,128)S(1)}, u32[]{:S(2)}, u32[]{:S(2)}) async-start(s32[8,4,9]{2,1,0:T(4,128)} %bitcast.13), calls=%async_computation | async-start | bytes 32768 | tf_op jit(solution)/shard_map/all_to_all | solution.py:70
  268.6 195.4 %all-to-all-start.1 = ((bf16[32,8,128,128]{3,2,1,0:T(8,128)(2,1)}), bf16[32,8,128,128]{3,2,1,0:T(8,128)(2,1)}, u32[]{:S(2)}, u32[]{:S(2)}) async-start(bf16[32,8,128,128]{3,2,1,0:T(8,128)(2,1)} %copy.25), calls=%async_computation.1 | async-start | bytes 16777216 | tf_op jit(solution)/shard_map/all_to_all | solution.py:69
where the time goes:
time: 544 us; the launch traced here: 539 us
  waiting for transfers between devices  238 us (44%)
  other arithmetic  93 us (17%)
  matrix products  91.1 us (17%)
  local copies, waits for them, and re-layouts  88.6 us (16%)
  starting transfers between devices  27.8 us (5%)
    all_to_all x1, waiting for transfers between devices, shards(): lax.all_to_all(send_tiles, 'gy', split_axis=0, concat_axis=0, tiled=True)  184 us
    scatter-add x1, other arithmetic, shards(): jax.ops.segment_sum(flat_contrib, segment_ids.reshape(-1), num_segments=c...  53.3 us
    ppermute x2, waiting for transfers between devices, extended(): lax.ppermute(lax.slice_in_dim(block, block.shape[dim] - width, None, axis...  51.4 us
    gather x16, local copies, waits for them, and re-layouts, one_row(): far_tiles = jnp.take(p_table, column_row, axis=0)  48.9 us
    dot_general x16, matrix products, one_row(): jnp.einsum('kf,kac->fac', picker, products, precision=lax.Precision.HIGHEST)  28 us
    dot_general x16, matrix products, one_row(): jnp.einsum('ba,fbc->fac', p_row, summed, preferred_element_type=jnp.float32)  27.7 us
    dot_general x16, matrix products, one_row(): jnp.einsum('kab,kbc->kac', a_row, far_tiles, preferred_element_type=jnp.f...  26 us
    and x16, other arithmetic, one_row(): far_tiles = jnp.take(p_table, column_row, axis=0)  11.3 us
  transfers between devices with their start and end apart: 6, of which 4 were waited for; matrix products, arithmetic and copies ran while one was open for 37% of the time, Pallas kernels for 0%

commit v1 on v0

--- a/solution.py
+++ b/solution.py
@@ -5,6 +5,22 @@
 
 KC = 27
 AGG = 4
+
+
+def exchange_in_pairs(x, axis, split, join):
+    ways, here = (lax.axis_size(axis), lax.axis_index(axis))
+    width = x.shape[split] // ways
+    dims = list(x.shape)
+    dims[split] = width
+    height = dims[join]
+    dims[join] = height * ways
+    full = jnp.zeros(dims, x.dtype)
+    for mask in range(ways):
+        part = lax.dynamic_slice_in_dim(x, (here ^ mask) * width, width, axis=split)
+        if mask:
+            part = lax.ppermute(part, axis, [(d, d ^ mask) for d in range(ways)])
+        full = lax.dynamic_update_slice_in_dim(full, part, (here ^ mask) * height, axis=join)
+    return full
 
 
 def extended(block, sides, width):
@@ -66,7 +82,7 @@
         "sr,rfab->sfab", selector.astype(jnp.bfloat16), partials, preferred_element_type=jnp.float32
     ).astype(jnp.bfloat16)
     recv_contrib, recv_meta = (
-        lax.all_to_all(send_tiles, "gy", split_axis=0, concat_axis=0, tiled=True),
+        exchange_in_pairs(send_tiles, "gy", 0, 0),
         lax.all_to_all(meta_sent, "gy", split_axis=0, concat_axis=0, tiled=True),
     )
     recv_row = recv_meta[:, 0] - 1

time: 544 us -> 558 us (1.026)
  the two profiles are of different devices: /device:TPU:0 before, /device:TPU:16 now
where the time goes in v1:
time: 558 us; the launch traced here: 553 us
  waiting for transfers between devices  227 us (41%)
  local copies, waits for them, and re-layouts  104 us (19%)
  other arithmetic  91.7 us (16%)
  matrix products  86.5 us (16%)
  blocking collectives  24.9 us (4%)
  starting transfers between devices  19.1 us (3%)
    ppermute x7, waiting for transfers between devices, exchange_in_pairs(): part = lax.ppermute(part, axis, [(d, d ^ mask) for d in range(ways)])  158 us
    ppermute x2, waiting for transfers between devices, extended(): lax.ppermute(lax.slice_in_dim(block, block.shape[dim] - width, None, axis...  59.4 us
    scatter-add x1, other arithmetic, shards(): jax.ops.segment_sum(flat_contrib, segment_ids.reshape(-1), num_segments=c...  52.6 us
    gather x16, local copies, waits for them, and re-layouts, one_row(): far_tiles = jnp.take(p_table, column_row, axis=0)  48.9 us
    dot_general x16, matrix products, one_row(): jnp.einsum('kf,kac->fac', picker, products, precision=lax.Precision.HIGHEST)  28 us
    dot_general x16, matrix products, one_row(): jnp.einsum('ba,fbc->fac', p_row, summed, preferred_element_type=jnp.float32)  27.6 us
    dot_general x16, matrix products, one_row(): jnp.einsum('kab,kbc->kac', a_row, far_tiles, preferred_element_type=jnp.f...  26.1 us
    all_to_all x1, blocking collectives, shards(): lax.all_to_all(meta_sent, 'gy', split_axis=0, concat_axis=0, tiled=True)  24.9 us
  transfers between devices with their start and end apart: 11, of which 9 were waited for; matrix products, arithmetic and copies ran while one was open for 4% of the time, Pallas kernels for 0%

profile of v1, /device:TPU:16, one launch (start us, length us, event | category | flops | bytes accessed | tf_op | source)
XLA Modules:
  0.0 553.1 jit_solution(5568995152177312878)
XLA Ops:
  0.0 1.8 collective-permute-start
  4.6 2.4 collective-permute-done.1
  7.1 3.4 collective-permute-start.2
  10.5 3.3 collective-permute-start.3
  15.5 59.1 %collective-permute-done.2 = bf16[3,1,16,128,128]{4,3,2,1,0:T(8,128)(2,1)S(1)} collective-permute-done((bf16[3,1,16,128,128]{4,3,2,1,0:T(8,128)(2,1)S(1)}, bf16[3,1,16,128,128]{4,3,2,1,0:T(8,128)(2,1)S(1)}, u32[]{:S(2)}, u32[]{:S(2)}) %collective-permute-start.2) | collective-permute-done | bytes 1572896 | tf_op jit(solution)/shard_map/ppermute | solution.py:31
  74.5 6.4 %collective-permute-done.3 = bf16[3,1,16,128,128]{4,3,2,1,0:T(8,128)(2,1)} collective-permute-done((bf16[3,1,16,128,128]{4,3,2,1,0:T(8,128)(2,1)S(1)}, bf16[3,1,16,128,128]{4,3,2,1,0:T(8,128)(2,1)}, u32[]{:S(2)}, u32[]{:S(2)}) %collective-permute-start.3) | collective-permute-done | bytes 1572896 | tf_op jit(solution)/shard_map/ppermute | solution.py:34
  80.9 3.6 pad_maximum_fusion
  84.5 164.4 %while.10 = (s32[]{:T(128)}, bf16[16,8,128,128]{2,3,1,0:T(8,128)(2,1)}, s32[16,27]{1,0:T(8,128)}, bf16[16,27,128,128]{3,2,1,0:T(8,128)(2,1)}, s32[16,27]{1,0:T(8...) while((s32[]{:T(128)}, bf16[16,8,128,128]{2,3,1,0:T(8,128)(2,1)}, ...), condition=%wide.region_2.3_spmd, body=%wide.region_1.2_spmd.sunk | while | flops 189973952 | bytes 7903735 | solution.py:70
  85.2 3.1 gather_fusion
  91.3 1.7 fusion.58
  95.4 3.1 gather_fusion
  101.5 1.7 fusion.58
  105.7 3.1 gather_fusion
  111.8 1.7 fusion.58
  116.0 3.1 gather_fusion
  122.1 1.7 fusion.58
  126.2 3.1 gather_fusion
  132.3 1.7 fusion.58
  136.5 3.1 gather_fusion
  142.6 1.7 fusion.58
  144.4 1.7 fusion.59
  146.8 3.1 gather_fusion
  152.9 1.7 fusion.58
  154.7 1.7 fusion.59
  157.1 3.1 gather_fusion
  163.2 1.7 fusion.58
  164.9 1.7 fusion.59
  167.4 3.1 gather_fusion
  173.5 1.7 fusion.58
  175.2 1.7 fusion.59
  177.7 3.1 gather_fusion
  183.8 1.7 fusion.58
  187.9 3.1 gather_fusion
  194.0 1.7 fusion.58
  198.2 3.1 gather_fusion
  204.3 1.7 fusion.58
  206.1 1.8 fusion.59
  208.5 3.1 gather_fusion
  214.6 1.7 fusion.58
  218.8 3.1 gather_fusion
  224.9 1.7 fusion.58
  229.1 3.1 gather_fusion
  235.2 1.7 fusion.58
  239.3 3.1 gather_fusion
  245.4 1.7 fusion.58
  248.9 6.7 %copy.33 = bf16[16,8,128,128]{3,0,2,1:T(8,128)(2,1)} copy(bf16[16,8,128,128]{2,3,1,0:T(8,128)(2,1)} %get-tuple-element.42) | data formatting | bytes 8388608 | tf_op jit(solution)/shard_map/while | solution.py:70
  255.6 4.6 convolution_convert_fusion.1
  260.3 6.1 %constant_dynamic-slice_fusion.2 = (bf16[4,8,128,128]{3,0,2,1:T(4,128)(2,1)S(1)}, bf16[4,8,128,128]{3,0,2,1:T(4,128)(2,1)S(1)}, bf16[4,8,128,128]{3,0,2,1:T(4,12...) fusion(bf16[32,8,128,128]{3,0,2,1:T(8,128)(2,1)S(1)} %convoluti, ...), kind=kLoop, calls=%fused_computation.62 | loop fusion | bytes 16777248 | tf_op jit(solution)/shard_map/dynamic_slice | solution.py:19
  268.3 24.9 %all_to_all.12 = s32[8,4,9]{2,1,0:T(4,128)S(1)} all-to-all(s32[8,4,9]{2,1,0:T(4,128)S(1)} %bitcast.76), channel_id=1, replica_groups=mesh['gx'=4,'gy'=8] {'gy'}, dimensions={0} | all-to-all | bytes 2304 | tf_op jit(solution)/shard_map/all_to_all | solution.py:86
  293.4 1.7 collective-permute-start.6
  296.7 2.5 collective-permute-start.8
  299.2 5.3 broadcast_in_dim.52
  307.1 2.5 copy_dynamic-update-slice_fusion.6
  310.3 2.5 copy_dynamic-update-slice_fusion.5
  312.8 26.1 %collective-permute-done.6 = bf16[4,8,128,128]{3,0,2,1:T(4,128)(2,1)} collective-permute-done((bf16[4,8,128,128]{3,0,2,1:T(4,128)(2,1)}, bf16[4,8,128,128]{3,0,2,1:T(4,128)(2,1)}, u32[]{:S(2)}, u32[]{:S(2)}) %collective-permute-start.6) | collective-permute-done | bytes 1048608 | tf_op jit(solution)/shard_map/ppermute | solution.py:21
  338.8 2.5 copy_dynamic-update-slice_fusion.4
  341.3 69.1 %collective-permute-done.7 = bf16[4,8,128,128]{3,0,2,1:T(4,128)(2,1)S(1)} collective-permute-done((bf16[4,8,128,128]{3,0,2,1:T(4,128)(2,1)}, bf16[4,8,128,128]{3,0,2,1:T(4,128)(2,1)S(1)}, u32[]{:S(2)}, u32[]{:S(2)}) %collective-permute-start.7) | collective-permute-done | bytes 1048608 | tf_op jit(solution)/shard_map/ppermute | solution.py:21
  411.7 21.2 %collective-permute-done.8 = bf16[4,8,128,128]{3,0,2,1:T(4,128)(2,1)S(1)} collective-permute-done((bf16[4,8,128,128]{3,0,2,1:T(4,128)(2,1)}, bf16[4,8,128,128]{3,0,2,1:T(4,128)(2,1)S(1)}, u32[]{:S(2)}, u32[]{:S(2)}) %collective-permute-start.8) | collective-permute-done | bytes 1048608 | tf_op jit(solution)/shard_map/ppermute | solution.py:21
  434.2 22.1 %collective-permute-done.9 = bf16[4,8,128,128]{3,0,2,1:T(4,128)(2,1)S(1)} collective-permute-done((bf16[4,8,128,128]{3,0,2,1:T(4,128)(2,1)S(1)}, bf16[4,8,128,128]{3,0,2,1:T(4,128)(2,1)S(1)}, u32[]{:S(2)}, u32[]{:S(2)}) %collective-permute-start.9) | collective-permute-done | bytes 1048608 | tf_op jit(solution)/shard_map/ppermute | solution.py:21
  457.5 19.8 %collective-permute-done.10 = bf16[4,8,128,128]{3,0,2,1:T(4,128)(2,1)S(1)} collective-permute-done((bf16[4,8,128,128]{3,0,2,1:T(4,128)(2,1)S(1)}, bf16[4,8,128,128]{3,0,2,1:T(4,128)(2,1)S(1)}, u32[]{:S(2)}, u32[]{:S(2)}) %collective-permute-start.10) | collective-permute-done | bytes 1048608 | tf_op jit(solution)/shard_map/ppermute | solution.py:21
  478.5 11.2 %bitcast_convert_fusion = f32[256,128,128]{2,1,0:T(8,128)} fusion(bf16[32,8,128,128]{3,2,1,0:T(8,128)(2,1)} %copy_dynamic-update-slice_fusion), kind=kLoop, calls=%fused_computation.31 | loop fusion | flops 4194304 | bytes 25165824 | tf_op jit(solution)/shard_map/convert_element_type | solution.py:92
  489.8 3.8 broadcast_in_dim.48
  493.6 52.6 %scatter_fusion = f32[109,128,128]{2,1,0:T(8,128)} fusion(f32[109,128,128]{2,1,0:T(8,128)} %broadcast_in_dim.48, s32[256]{0:T(256)S(1)} %reshape.186, f32[256,128,128]{2,1,0:T(8,128)} %bitcast_convert_fusion), kind=kCustom, calls=%fused_computation.1 | custom fusion | flops 4194304 | bytes 50332672 | tf_op jit(solution)/shard_map/scatter-add | solution.py:95
  546.2 6.9 %slice.16 = f32[108,128,128]{2,1,0:T(8,128)} slice(f32[109,128,128]{2,1,0:T(8,128)} %scatter_fusion), slice={[0:108], [0:128], [0:128]} | slice | bytes 14155776 | tf_op jit(solution)/shard_map/slice | solution.py:98
  (122 shorter events, 95.0 us)
Async XLA Ops:
  0.0 3.5 collective-permute-start
  1.8 5.3 collective-permute-start.1
  7.1 67.4 %collective-permute-start.2 = (bf16[3,1,16,128,128]{4,3,2,1,0:T(8,128)(2,1)S(1)}, bf16[3,1,16,128,128]{4,3,2,1,0:T(8,128)(2,1)S(1)}, u32[]{:S(2)}, u32[]{:S(2)}) collective-permute-start(bf16[3,1,16,128,128]{4,3,2,1,0:T(8,128)(2,1)S(1)} %constant_dynamic-update-slice_fusion), channel_id=1, source_target_pairs={{0,1},{1,2},{2,3},{3,4},{4,5},{5,6},{6,7},{8,9},{9,10},{10,11},{11... | collective-permute-start | bytes 4718600 | tf_op jit(solution)/shard_map/ppermute | solution.py:31
  10.5 70.4 %collective-permute-start.3 = (bf16[3,1,16,128,128]{4,3,2,1,0:T(8,128)(2,1)S(1)}, bf16[3,1,16,128,128]{4,3,2,1,0:T(8,128)(2,1)}, u32[]{:S(2)}, u32[]{:S(2)}) collective-permute-start(bf16[3,1,16,128,128]{4,3,2,1,0:T(8,128)(2,1)S(1)} %constant_dynamic-update-slice_fusion), channel_id=1, source_target_pairs={{1,0},{2,1},{3,2},{4,3},{5,4},{6,5},{7,6},{9,8},{10,9},{11,10},{12... | collective-permute-start | bytes 4718600 | tf_op jit(solution)/shard_map/ppermute | solution.py:34
  260.2 6.1 %copy-start.1 = (s32[1,1,16]{2,1,0:T(1,128)S(1)}, s32[1,1,16]{2,1,0:T(1,128)}, u32[]{:S(2)}) copy-start(s32[1,1,16]{2,1,0:T(1,128)} %param.13) | copy-start | bytes 196
  260.2 7.7 %copy-start = (s32[1,1,16,8]{2,3,1,0:T(8,128)S(1)}, s32[1,1,16,8]{2,3,1,0:T(8,128)}, u32[]{:S(2)}) copy-start(s32[1,1,16,8]{2,3,1,0:T(8,128)} %param.12) | copy-start | bytes 1540
  266.3 39.4 %collective-permute-start.4 = (bf16[4,8,128,128]{3,0,2,1:T(4,128)(2,1)}, bf16[4,8,128,128]{3,0,2,1:T(4,128)(2,1)}, u32[]{:S(2)}, u32[]{:S(2)}) collective-permute-start(bf16[4,8,128,128]{3,0,2,1:T(4,128)(2,1)} %get-tuple-element.63), channel_id=1, source_target_pairs={{0,1},{1,0},{2,3},{3,2},{4,5},{5,4},{6,7},{7,6},{8,9},{9,8},{10,11... | collective-permute-start | bytes 3145736 | tf_op jit(solution)/shard_map/ppermute | solution.py:21
  266.3 43.2 %collective-permute-start.5 = (bf16[4,8,128,128]{3,0,2,1:T(4,128)(2,1)}, bf16[4,8,128,128]{3,0,2,1:T(4,128)(2,1)}, u32[]{:S(2)}, u32[]{:S(2)}) collective-permute-start(bf16[4,8,128,128]{3,0,2,1:T(4,128)(2,1)} %get-tuple-element.62), channel_id=1, source_target_pairs={{0,2},{1,3},{2,0},{3,1},{4,6},{5,7},{6,4},{7,5},{8,10},{9,11},{10,... | collective-permute-start | bytes 3145736 | tf_op jit(solution)/shard_map/ppermute | solution.py:21
  293.4 45.4 %collective-permute-start.6 = (bf16[4,8,128,128]{3,0,2,1:T(4,128)(2,1)}, bf16[4,8,128,128]{3,0,2,1:T(4,128)(2,1)}, u32[]{:S(2)}, u32[]{:S(2)}) collective-permute-start(bf16[4,8,128,128]{3,0,2,1:T(4,128)(2,1)} %get-tuple-element.61), channel_id=1, source_target_pairs={{0,3},{1,2},{2,1},{3,0},{4,7},{5,6},{6,5},{7,4},{8,11},{9,10},{10,... | collective-permute-start | bytes 3145736 | tf_op jit(solution)/shard_map/ppermute | solution.py:21
  295.3 115.1 %collective-permute-start.7 = (bf16[4,8,128,128]{3,0,2,1:T(4,128)(2,1)}, bf16[4,8,128,128]{3,0,2,1:T(4,128)(2,1)S(1)}, u32[]{:S(2)}, u32[]{:S(2)}) collective-permute-start(bf16[4,8,128,128]{3,0,2,1:T(4,128)(2,1)} %get-tuple-element.60), channel_id=1, source_target_pairs={{0,4},{1,5},{2,6},{3,7},{4,0},{5,1},{6,2},{7,3},{8,12},{9,13},{10,... | collective-permute-start | bytes 3145736 | tf_op jit(solution)/shard_map/ppermute | solution.py:21
  296.7 136.2 %collective-permute-start.8 = (bf16[4,8,128,128]{3,0,2,1:T(4,128)(2,1)}, bf16[4,8,128,128]{3,0,2,1:T(4,128)(2,1)S(1)}, u32[]{:S(2)}, u32[]{:S(2)}) collective-permute-start(bf16[4,8,128,128]{3,0,2,1:T(4,128)(2,1)} %get-tuple-element.59), channel_id=1, source_target_pairs={{0,5},{1,4},{2,7},{3,6},{4,1},{5,0},{6,3},{7,2},{8,13},{9,12},{10,... | collective-permute-start | bytes 3145736 | tf_op jit(solution)/shard_map/ppermute | solution.py:21
  305.7 150.5 %collective-permute-start.9 = (bf16[4,8,128,128]{3,0,2,1:T(4,128)(2,1)S(1)}, bf16[4,8,128,128]{3,0,2,1:T(4,128)(2,1)S(1)}, u32[]{:S(2)}, u32[]{:S(2)}) collective-permute-start(bf16[4,8,128,128]{3,0,2,1:T(4,128)(2,1)S(1)} %get-tuple-element.58), channel_id=1, source_target_pairs={{0,6},{1,7},{2,4},{3,5},{4,2},{5,3},{6,0},{7,1},{8,14},{9,15},{10,... | collective-permute-start | bytes 3145736 | tf_op jit(solution)/shard_map/ppermute | solution.py:21
  309.6 167.7 %collective-permute-start.10 = (bf16[4,8,128,128]{3,0,2,1:T(4,128)(2,1)S(1)}, bf16[4,8,128,128]{3,0,2,1:T(4,128)(2,1)S(1)}, u32[]{:S(2)}, u32[]{:S(2)}) collective-permute-start(bf16[4,8,128,128]{3,0,2,1:T(4,128)(2,1)S(1)} %get-tuple-element.57), channel_id=1, source_target_pairs={{0,7},{1,6},{2,5},{3,4},{4,3},{5,2},{6,1},{7,0},{8,15},{9,14},{10,... | collective-permute-start | bytes 3145736 | tf_op jit(solution)/shard_map/ppermute | solution.py:21
